TPU v7x, 128 devices: a whole 4x4x4 slice. The times are simulated.
128 devices in a mesh: seq: 32 (over y, z, core), head: 4 (over x).
Axes of the slice: x: 4, y: 4, z: 4, core: 2. Of those that a mesh axis runs over, the one named last changes fastest.
Arguments:
- queries: bfloat16 [131072, 2048], P('seq', 'head'), may hold values from -6 to 6
- keys: bfloat16 [131072, 2048], P('seq', 'head'), may hold values from -0.59765625 to 0.59765625
- values: bfloat16 [131072, 2048], P('seq', 'head'), may hold values from -6 to 6
- norm_gain: float32 [2048], replicated, may hold values from 0.1 to 1.9
Outputs:
- normed: bfloat16 [131072, 2048], P(('seq', 'head'))
All inputs are finite; a program needn't handle non-finite values.
Results may differ from a plain program's by a relative error of at most 0.0058.
Values may be sent and summed in bfloat16 or wider, within the bound.
A program may use at most 128 MiB of HBM per device.

v0:
```python
import jax
import jax.numpy as jnp
from jax import lax
from jax.sharding import PartitionSpec as P

DH = 128
BLK = 512


def add_lower(piece, mine):
    ranks = jnp.arange(piece.shape[0], dtype=jnp.int32)
    keep = (ranks < mine).astype(jnp.float32)[:, None, None, None]
    return jnp.sum(piece * keep, axis=0)


def shards(queries, keys, values, norm_gain):
    rows, width = queries.shape
    heads = width // DH
    blocks = rows // BLK
    query_rows = queries.reshape(blocks, BLK, heads, DH)
    key_rows = keys.reshape(blocks, BLK, heads, DH)
    value_rows = values.reshape(blocks, BLK, heads, DH)
    block_state = jnp.einsum(
        "nbhd,nbhe->nhde", key_rows, value_rows, preferred_element_type=jnp.float32
    )
    total = jnp.sum(block_state, axis=0)
    mine = lax.axis_index("seq")
    before = add_lower(lax.all_gather(total[None], "seq", axis=0, tiled=True), mine)
    running = jnp.cumsum(block_state, axis=0)
    within = jnp.concatenate([jnp.zeros_like(block_state[:1]), running[:-1]], axis=0)
    prefix_low = (before[None] + within).astype(jnp.bfloat16)
    inter = jnp.einsum(
        "nbhd,nhde->nbhe", query_rows, prefix_low, preferred_element_type=jnp.float32
    )
    scores = jnp.einsum("nbhd,nchd->nhbc", query_rows, key_rows, preferred_element_type=jnp.float32)
    causal = jnp.arange(BLK)[:, None] >= jnp.arange(BLK)[None, :]
    scores = jnp.where(causal[None, None], scores, jnp.zeros_like(scores)).astype(jnp.bfloat16)
    intra = jnp.einsum("nhbc,nche->nbhe", scores, value_rows, preferred_element_type=jnp.float32)
    attention = (inter + intra).astype(jnp.bfloat16).reshape(rows, width)
    regrouped = lax.all_to_all(attention, "head", split_axis=0, concat_axis=1, tiled=True)
    widened = regrouped.astype(jnp.float32)
    meansq = jnp.mean(widened * widened, axis=-1, keepdims=True)
    return (widened * lax.rsqrt(meansq + 1e-06) * norm_gain[None, :]).astype(jnp.bfloat16)


def solution(mesh):
    return jax.shard_map(
        shards,
        mesh=mesh,
        in_specs=(P("seq", "head"), P("seq", "head"), P("seq", "head"), P()),
        out_specs=P(("seq", "head"), None),
        check_vma=False,
    )
```

profile of v0, /device:TPU:1, one launch (start us, length us, event | category | flops | bytes accessed | tf_op | source)
XLA Modules:
  0.0 208.3 jit_solution(7834512053648835471)
XLA Ops:
  6.5 0.0 all-gather.3.cloned.1.call-start
  6.5 6.9 %reshape.43 = bf16[8,512,4,128]{3,2,1,0:T(4,128)(2,1)} reshape(bf16[4096,512]{1,0:T(8,128)(2,1)} %param.5) | data formatting | bytes 8388608 | tf_op jit(solution)/shard_map/reshape | solution.py:21
  13.4 6.9 %reshape.44 = bf16[8,512,4,128]{3,2,1,0:T(4,128)(2,1)} reshape(bf16[4096,512]{1,0:T(8,128)(2,1)} %param.6) | data formatting | bytes 8388608 | tf_op jit(solution)/shard_map/reshape | solution.py:22
  20.4 5.9 %fusion.28 = (f32[4,128,128]{2,1,0:T(8,128)}, f32[8,4,128,128]{3,2,1,0:T(8,128)S(1)}) fusion(bf16[8,512,4,128]{3,2,1,0:T(4,128)(2,1)} %reshape.44, bf16[8,512,4,128]{3,2,1,0:T(4,128)(2,1)} %reshape.43), kind=kOutput, calls=%fused_computation.29 | convolution fusion | flops 537329664 | bytes 10747904 | tf_op jit(solution)/shard_map/nbhd,nbhe->nhde/dot_general | solution.py:23
  26.3 0.0 all-gather.3.cloned.1.call-update
  26.3 6.9 %reshape.45 = bf16[8,512,4,128]{3,2,1,0:T(4,128)(2,1)} reshape(bf16[4096,512]{1,0:T(8,128)(2,1)} %param.4) | data formatting | bytes 8388608 | tf_op jit(solution)/shard_map/reshape | solution.py:20
  33.2 1.9 fusion.29
  35.1 0.2 slice.4
  35.3 0.1 iota_compare_fusion
  35.4 47.7 %all-gather.3.cloned.1.call-done = f32[128,128,128]{2,1,0:T(8,128)} async-done(((f32[4,128,128]{2,1,0:T(8,128)}), f32[128,128,128]{2,1,0:T(8,128)}) %all-gather.3.cloned.1.call-update) | async-done | bytes 8388624 | tf_op jit(solution)/shard_map/all_gather | solution.py:28
  83.1 0.0 copy-start
  83.1 4.7 %multiply_reduce_fusion = f32[4,128,128]{2,1,0:T(8,128)S(1)} fusion(f32[32,4,128,128]{3,2,1,0:T(8,128)} %bitcast.16, f32[32]{0:T(128)S(1)} %compare_convert_fusion), kind=kLoop, calls=%fused_computation.13 | loop fusion | flops 4128768 | bytes 8650880 | tf_op jit(solution)/shard_map/reduce_sum | solution.py:13
  87.8 0.0 copy-done
  87.8 4.6 %fusion.15 = f32[8,4,128,512]{3,2,1,0:T(8,128)} fusion(bf16[8,512,4,128]{3,2,1,0:T(4,128)(2,1)S(1)} %copy-done, f32[7,4,128,128]{3,2,1,0:T(8,128)S(1)} %slice.4, f32[4,128,128]{2,1,0:T(8,128)S(1)} %multiply_reduce_fusion), kind=kOutput, calls=%fused_computation.18 | convolution fusion | flops 537919488 | bytes 14680064 | tf_op jit(solution)/shard_map/nbhd,nhde->nbhe/dot_general | solution.py:32
  92.4 16.4 %fusion.8 = bf16[8,512,4,128]{1,3,2,0:T(8,128)(2,1)} fusion(f32[8,4,128,512]{3,2,1,0:T(8,128)} %fusion.15, bf16[8,512,4,128]{3,2,1,0:T(4,128)(2,1)} %reshape.44, pred[512,512]{1,0:T(8,128)(4,1)S(1)} %iota_compare_fusion, bf16[8,512,4,128]{3,2,1,0:T(4,128)(2,1)} %reshape.43, bf16[8,512,4,128]{3,2,1,0:T(4,128)(2,1)} %reshape.45), kind=kOutput, calls=%fused_computation.12 | convolution fusion | flops 4315938816 | bytes 25427968 | tf_op jit(solution)/shard_map/nhbc,nche->nbhe/dot_general | solution.py:38
  108.9 7.4 %copy.37 = bf16[8,512,4,128]{3,2,1,0:T(4,128)(2,1)} copy(bf16[8,512,4,128]{1,3,2,0:T(8,128)(2,1)} %fusion.8) | data formatting | bytes 8388608 | tf_op jit(solution)/shard_map/convert_element_type | solution.py:39
  116.3 7.2 %all_to_all.10 = bf16[4,1024,512]{2,1,0:T(8,128)(2,1)} reshape(bf16[8,512,4,128]{3,2,1,0:T(4,128)(2,1)} %copy.37) | data formatting | bytes 8388608 | tf_op jit(solution)/shard_map/all_to_all | solution.py:40
  123.5 52.3 %all_to_all.13 = bf16[4,1024,512]{2,1,0:T(8,128)(2,1)S(1)} all-to-all(bf16[4,1024,512]{2,1,0:T(8,128)(2,1)} %all_to_all.10), channel_id=1, replica_groups=mesh['seq'=32,'head'=4] {'head'}, dimensions={0} | all-to-all | bytes 8388608 | tf_op jit(solution)/shard_map/all_to_all | solution.py:40
  175.8 0.9 fusion.5
  176.7 4.4 %convert_bitcast_fusion = f32[1024,4,512]{2,0,1:T(8,128)} fusion(bf16[4,1024,512]{2,1,0:T(8,128)(2,1)S(1)} %all_to_all.13), kind=kLoop, calls=%fused_computation.6 | loop fusion | flops 2097152 | bytes 12582912 | tf_op jit(solution)/shard_map/convert_element_type | solution.py:41
  181.1 0.0 copy-start.1
  181.1 8.7 %copy.38 = f32[1024,4,512]{0,2,1:T(8,128)} copy(f32[1024,4,512]{2,0,1:T(8,128)} %convert_bitcast_fusion) | data formatting | bytes 16777216 | tf_op jit(solution)/shard_map/convert_element_type | solution.py:41
  189.9 0.0 copy-done.1
  189.9 5.2 %fusion.7 = bf16[1024,2048]{0,1:T(8,128)(2,1)} fusion(f32[1024,4,512]{0,2,1:T(8,128)} %copy.38, f32[2048]{0:T(1024)S(1)} %copy-done.1, f32[1024]{0:T(1024)S(1)} %add_rsqrt_fusion), kind=kLoop, calls=%fused_computation.10 | loop fusion | flops 6291456 | bytes 12595200 | tf_op jit(solution)/shard_map/convert_element_type | solution.py:43
  195.1 6.4 %copy.39 = bf16[1024,2048]{1,0:T(8,128)(2,1)} copy(bf16[1024,2048]{0,1:T(8,128)(2,1)} %fusion.7) | data formatting | bytes 8388608 | tf_op jit(solution)/shard_map/convert_element_type | solution.py:43
  (2 shorter events, 0.0 us)
Async XLA Ops:
  6.5 76.6 %all-gather.3.cloned.1.call-start = ((), (), s32[]{:S(2)}) async-start(), calls=%async_computation.1 | async-start | bytes 8650752 | tf_op jit(solution)/shard_map/all_gather | solution.py:28
  83.1 4.7 %copy-start = (bf16[8,512,4,128]{3,2,1,0:T(4,128)(2,1)S(1)}, bf16[8,512,4,128]{3,2,1,0:T(4,128)(2,1)}, u32[]{:S(2)}) copy-start(bf16[8,512,4,128]{3,2,1,0:T(4,128)(2,1)} %reshape.45) | copy-start | bytes 12582916
  181.1 8.8 %copy-start.1 = (f32[2048]{0:T(1024)S(1)}, f32[2048]{0:T(1024)}, u32[]{:S(2)}) copy-start(f32[2048]{0:T(1024)} %param.7) | copy-start | bytes 24580
Sparse Core Ops, SparseCore 0:
  26.4 56.6 all-gather.2
where the time goes:
time: 210 us; the launch traced here: 208 us
  blocking collectives  52.3 us (25%)
  local copies, waits for them, and re-layouts  50.7 us (24%)
  waiting for transfers between devices  47.7 us (23%)
  matrix products  27 us (13%)
  other arithmetic  17.1 us (8%)
  between operations  13.5 us (6%)
    all_to_all x1, blocking collectives, shards(): lax.all_to_all(attention, 'head', split_axis=0, concat_axis=1, tiled=True)  52.3 us
    all_gather x1, waiting for transfers between devices, shards(): lax.all_gather(total[None], 'seq', axis=0, tiled=True)  47.7 us
    dot_general x1, matrix products, shards(): jnp.einsum('nhbc,nche->nbhe', scores, value_rows, preferred_element_type=...  16.4 us
    convert_element_type x1, local copies, waits for them, and re-layouts, shards(): widened = regrouped.astype(jnp.float32)  8.75 us
    convert_element_type x1, local copies, waits for them, and re-layouts, shards(): attention = (inter + intra).astype(jnp.bfloat16).reshape(rows, width)  7.44 us
    all_to_all x1, local copies, waits for them, and re-layouts, shards(): lax.all_to_all(attention, 'head', split_axis=0, concat_axis=1, tiled=True)  7.21 us
    reshape x1, local copies, waits for them, and re-layouts, shards(): value_rows = values.reshape(blocks, BLK, heads, DH)  6.93 us
    reshape x1, local copies, waits for them, and re-layouts, shards(): key_rows = keys.reshape(blocks, BLK, heads, DH)  6.91 us
  transfers between devices with their start and end apart: 1, of which 1 were waited for; matrix products, arithmetic and copies ran while one was open for 4% of the time, Pallas kernels for 0%

commit v1 on v0

--- a/solution.py
+++ b/solution.py
@@ -25,7 +25,18 @@
     )
     total = jnp.sum(block_state, axis=0)
     mine = lax.axis_index("seq")
-    before = add_lower(lax.all_gather(total[None], "seq", axis=0, tiled=True), mine)
+    before = add_lower(
+        jnp.concatenate(
+            lax.all_to_all(
+                jnp.stack([total[None]] * lax.axis_size("seq")),
+                axis_name="seq",
+                split_axis=0,
+                concat_axis=0,
+            ),
+            axis=0,
+        ),
+        mine,
+    )
     running = jnp.cumsum(block_state, axis=0)
     within = jnp.concatenate([jnp.zeros_like(block_state[:1]), running[:-1]], axis=0)
     prefix_low = (before[None] + within).astype(jnp.bfloat16)

time: 210 us -> 282 us (1.34)
  the two profiles are of different devices: /device:TPU:1 before, /device:TPU:32 now
where the time goes in v1:
time: 282 us; the launch traced here: 280 us
  waiting for transfers between devices  115 us (41%)
  local copies, waits for them, and re-layouts  57.1 us (20%)
  blocking collectives  52.9 us (19%)
  matrix products  27.6 us (10%)
  other arithmetic  19.2 us (7%)
  starting transfers between devices  8.26 us (3%)
    all_to_all x1, waiting for transfers between devices, shards(): lax.all_to_all(jnp.stack([total[None]] * lax.axis_size('seq')), axis_name...  115 us
    all_to_all x1, blocking collectives, shards(): lax.all_to_all(attention, 'head', split_axis=0, concat_axis=1, tiled=True)  52.9 us
    dot_general x1, matrix products, shards(): jnp.einsum('nhbc,nche->nbhe', scores, value_rows, preferred_element_type=...  16.4 us
    convert_element_type x1, local copies, waits for them, and re-layouts, shards(): widened = regrouped.astype(jnp.float32)  8.73 us
    all_to_all x1, starting transfers between devices, shards(): lax.all_to_all(jnp.stack([total[None]] * lax.axis_size('seq')), axis_name...  8.26 us
    convert_element_type x1, local copies, waits for them, and re-layouts, shards(): attention = (inter + intra).astype(jnp.bfloat16).reshape(rows, width)  7.44 us
    all_to_all x1, local copies, waits for them, and re-layouts, shards(): lax.all_to_all(attention, 'head', split_axis=0, concat_axis=1, tiled=True)  7.21 us
    reshape x1, local copies, waits for them, and re-layouts, shards(): query_rows = queries.reshape(blocks, BLK, heads, DH)  7.13 us
  transfers between devices with their start and end apart: 1, of which 1 were waited for; matrix products, arithmetic and copies ran while one was open for 3% of the time, Pallas kernels for 0%

profile of v1, /device:TPU:32, one launch (start us, length us, event | category | flops | bytes accessed | tf_op | source)
XLA Modules:
  0.0 280.3 jit_solution(17400943609982083812)
XLA Ops:
  0.0 6.9 %reshape.48 = bf16[8,512,4,128]{3,2,1,0:T(4,128)(2,1)} reshape(bf16[4096,512]{1,0:T(8,128)(2,1)} %param.5) | data formatting | bytes 8388608 | tf_op jit(solution)/shard_map/reshape | solution.py:21
  6.9 6.9 %reshape.49 = bf16[8,512,4,128]{3,2,1,0:T(4,128)(2,1)} reshape(bf16[4096,512]{1,0:T(8,128)(2,1)} %param.6) | data formatting | bytes 8388608 | tf_op jit(solution)/shard_map/reshape | solution.py:22
  13.9 6.5 %fusion.29 = (f32[4,128,128]{2,1,0:T(8,128)S(1)}, f32[8,4,128,128]{3,2,1,0:T(8,128)}) fusion(bf16[8,512,4,128]{3,2,1,0:T(4,128)(2,1)} %reshape.49, bf16[8,512,4,128]{3,2,1,0:T(4,128)(2,1)} %reshape.48), kind=kOutput, calls=%fused_computation.30 | convolution fusion | flops 537329664 | bytes 10747904 | tf_op jit(solution)/shard_map/nbhd,nbhe->nhde/dot_general | solution.py:23
  20.4 4.3 %stack.3 = f32[32,1,4,128,128]{4,3,2,1,0:T(8,128)} broadcast(f32[4,128,128]{2,1,0:T(8,128)S(1)} %get-tuple-element.5), dimensions={2,3,4} | broadcast | bytes 8650752 | tf_op jit(solution)/shard_map/stack | solution.py:31
  24.6 8.3 %all-to-all-start = ((f32[32,1,4,128,128]{4,3,2,1,0:T(8,128)}), f32[32,1,4,128,128]{4,3,2,1,0:T(8,128)}, u32[]{:S(2)}, u32[]{:S(2)}) async-start(f32[32,1,4,128,128]{4,3,2,1,0:T(8,128)} %stack.3), calls=%async_computation | async-start | bytes 16777216 | tf_op jit(solution)/shard_map/all_to_all | solution.py:30
  32.9 1.8 fusion.30
  34.7 0.0 copy-start.2
  34.7 7.1 %reshape.51 = bf16[8,512,4,128]{3,2,1,0:T(4,128)(2,1)} reshape(bf16[4096,512]{1,0:T(8,128)(2,1)} %param.4) | data formatting | bytes 8388608 | tf_op jit(solution)/shard_map/reshape | solution.py:20
  41.8 0.0 copy-done.2
  41.8 0.1 iota_compare_fusion
  41.9 0.0 slice-start
  41.9 115.2 %all-to-all-done = f32[32,1,4,128,128]{4,3,2,1,0:T(8,128)} async-done(((f32[32,1,4,128,128]{4,3,2,1,0:T(8,128)}), f32[32,1,4,128,128]{4,3,2,1,0:T(8,128)}, u32[]{:S(2)}, u32[]{:S(2)}) %all-to-all-start) | async-done | bytes 8388640 | tf_op jit(solution)/shard_map/all_to_all | solution.py:30
  157.2 0.0 copy-start.1
  157.2 4.7 %fusion.9 = f32[4,128,128]{2,1,0:T(8,128)S(1)} fusion(f32[32,1,4,128,128]{4,3,2,1,0:T(8,128)} %all-to-all-done, f32[32]{0:T(128)S(1)} %compare_convert_fusion), kind=kLoop, calls=%fused_computation.14 | loop fusion | flops 4128768 | bytes 8650880 | tf_op jit(solution)/shard_map/reduce_sum | solution.py:13
  161.8 0.0 slice-done
  161.8 0.0 copy-done.1
  161.8 4.6 %fusion.16 = f32[8,4,128,512]{3,2,1,0:T(8,128)} fusion(bf16[8,512,4,128]{3,2,1,0:T(4,128)(2,1)S(1)} %copy-done.1, f32[7,4,128,128]{3,2,1,0:T(8,128)S(1)} %slice-done, f32[4,128,128]{2,1,0:T(8,128)S(1)} %fusion.9), kind=kOutput, calls=%fused_computation.19 | convolution fusion | flops 537919488 | bytes 14680064 | tf_op jit(solution)/shard_map/nbhd,nhde->nbhe/dot_general | solution.py:43
  166.5 16.4 %fusion.8 = bf16[8,512,4,128]{1,3,2,0:T(8,128)(2,1)} fusion(f32[8,4,128,512]{3,2,1,0:T(8,128)} %fusion.16, bf16[8,512,4,128]{3,2,1,0:T(4,128)(2,1)} %reshape.49, pred[512,512]{1,0:T(8,128)(4,1)S(1)} %iota_compare_fusion, bf16[8,512,4,128]{3,2,1,0:T(4,128)(2,1)} %reshape.48, bf16[8,512,4,128]{3,2,1,0:T(4,128)(2,1)} %reshape.51), kind=kOutput, calls=%fused_computation.12 | convolution fusion | flops 4315938816 | bytes 25427968 | tf_op jit(solution)/shard_map/nhbc,nche->nbhe/dot_general | solution.py:49
  182.9 7.4 %copy.48 = bf16[8,512,4,128]{3,2,1,0:T(4,128)(2,1)} copy(bf16[8,512,4,128]{1,3,2,0:T(8,128)(2,1)} %fusion.8) | data formatting | bytes 8388608 | tf_op jit(solution)/shard_map/convert_element_type | solution.py:50
  190.3 7.2 %all_to_all.14 = bf16[4,1024,512]{2,1,0:T(8,128)(2,1)} reshape(bf16[8,512,4,128]{3,2,1,0:T(4,128)(2,1)} %copy.48) | data formatting | bytes 8388608 | tf_op jit(solution)/shard_map/all_to_all | solution.py:51
  197.5 52.9 %all_to_all.18 = bf16[4,1024,512]{2,1,0:T(8,128)(2,1)S(1)} all-to-all(bf16[4,1024,512]{2,1,0:T(8,128)(2,1)} %all_to_all.14), channel_id=1, replica_groups=mesh['seq'=32,'head'=4] {'head'}, dimensions={0} | all-to-all | bytes 8388608 | tf_op jit(solution)/shard_map/all_to_all | solution.py:51
  250.4 0.0 copy-start
  250.4 2.0 copy-done
  252.4 4.4 %convert_bitcast_fusion = f32[1024,4,512]{2,0,1:T(8,128)} fusion(bf16[4,1024,512]{2,1,0:T(8,128)(2,1)S(1)} %all_to_all.18), kind=kLoop, calls=%fused_computation.6 | loop fusion | flops 2097152 | bytes 12582912 | tf_op jit(solution)/shard_map/convert_element_type | solution.py:52
  256.8 8.7 %copy.49 = f32[1024,4,512]{0,2,1:T(8,128)} copy(f32[1024,4,512]{2,0,1:T(8,128)} %convert_bitcast_fusion) | data formatting | bytes 16777216 | tf_op jit(solution)/shard_map/convert_element_type | solution.py:52
  265.6 0.0 copy-start.3
  265.6 3.1 %fusion.5 = f32[1024]{0:T(1024)S(1)} fusion(bf16[4,1024,512]{2,1,0:T(8,128)(2,1)} %copy-done), kind=kLoop, calls=%fused_computation.7 | loop fusion | flops 6290432 | bytes 4198400 | tf_op jit(solution)/shard_map/reduce_sum | solution.py:53
  268.7 0.0 copy-done.3
  268.7 5.2 %fusion.7 = bf16[1024,2048]{0,1:T(8,128)(2,1)} fusion(f32[1024,4,512]{0,2,1:T(8,128)} %copy.49, f32[2048]{0:T(1024)S(1)} %copy-done.3, f32[1024]{0:T(1024)S(1)} %add_rsqrt_fusion), kind=kLoop, calls=%fused_computation.10 | loop fusion | flops 6291456 | bytes 12595200 | tf_op jit(solution)/shard_map/convert_element_type | solution.py:54
  273.9 6.4 %copy.50 = bf16[1024,2048]{1,0:T(8,128)(2,1)} copy(bf16[1024,2048]{0,1:T(8,128)(2,1)} %fusion.7) | data formatting | bytes 8388608 | tf_op jit(solution)/shard_map/convert_element_type | solution.py:54
  (2 shorter events, 0.0 us)
Async XLA Ops:
  24.6 132.5 %all-to-all-start = ((f32[32,1,4,128,128]{4,3,2,1,0:T(8,128)}), f32[32,1,4,128,128]{4,3,2,1,0:T(8,128)}, u32[]{:S(2)}, u32[]{:S(2)}) async-start(f32[32,1,4,128,128]{4,3,2,1,0:T(8,128)} %stack.3), calls=%async_computation | async-start | bytes 16777216 | tf_op jit(solution)/shard_map/all_to_all | solution.py:30
  34.7 7.1 %copy-start.2 = (f32[8,4,128,128]{3,2,1,0:T(8,128)}, f32[8,4,128,128]{3,2,1,0:T(8,128)S(1)}, u32[]{:S(2)}) copy-start(f32[8,4,128,128]{3,2,1,0:T(8,128)S(1)} %fusion.30) | copy-start | bytes 6291460
  41.9 119.9 %slice-start = ((f32[8,4,128,128]{3,2,1,0:T(8,128)}), f32[7,4,128,128]{3,2,1,0:T(8,128)S(1)}, s32[]{:S(2)}) async-start(f32[8,4,128,128]{3,2,1,0:T(8,128)} %copy-done.2), calls=%async_computation.2 | async-start | bytes 3670016 | tf_op jit(solution)/shard_map/slice | solution.py:41
  157.2 4.7 %copy-start.1 = (bf16[8,512,4,128]{3,2,1,0:T(4,128)(2,1)S(1)}, bf16[8,512,4,128]{3,2,1,0:T(4,128)(2,1)}, u32[]{:S(2)}) copy-start(bf16[8,512,4,128]{3,2,1,0:T(4,128)(2,1)} %reshape.51) | copy-start | bytes 12582916
  250.4 2.0 copy-start
  265.6 3.1 %copy-start.3 = (f32[2048]{0:T(1024)S(1)}, f32[2048]{0:T(1024)}, u32[]{:S(2)}) copy-start(f32[2048]{0:T(1024)} %param.7) | copy-start | bytes 24580
